TPU v7x, 128 devices: a whole 4x4x4 slice. The times are simulated.
128 devices in a mesh: ta: 8 (over z_hi, y), ha: 2 (over core), wa: 8 (over z_lo, x).
Axes of the slice: x: 4, y: 4, z: 4 (z_hi: 2, z_lo: 2; z = z_hi * 2 + z_lo), core: 2. Of those that a mesh axis runs over, the one named last changes fastest.
Arguments:
- queries: bfloat16 [32, 32, 64, 768], P('ta', 'ha', 'wa'), may hold values from -64 to 64
- keys: bfloat16 [32, 32, 64, 768], P('ta', 'ha', 'wa'), may hold values from -4 to 4
- values: bfloat16 [32, 32, 64, 768], P('ta', 'ha', 'wa'), may hold values from -6 to 6
- text_keys: bfloat16 [256, 768], P(('ta', 'ha', 'wa')), may hold values from -5 to 5
- text_values: bfloat16 [256, 768], P(('ta', 'ha', 'wa')), may hold values from -6 to 6
Outputs:
- attended: bfloat16 [32, 32, 64, 768], P('ta', 'ha', 'wa')
All inputs are finite; a program needn't handle non-finite values.
Results may differ from a plain program's by a relative error of at most 0.0037.
Values may be sent and summed in bfloat16 or wider, within the bound.
No kernel may reach another device: no remote copies, remote signals or barrier semaphores. Data moves between devices by JAX's collectives and lax.ppermute only.
A program may use at most 192 MiB of HBM per device.

v0:
```python
import jax
import jax.numpy as jnp
from jax import lax
from jax.sharding import PartitionSpec as P

HEADS = 6
TILE_T = 4
TILE_H = 8
TILE_W = 8


def extended(value, sides, width):
    for axis, dim in sides:
        size, length = (lax.axis_size(axis), value.shape[dim])
        up = [(i, (i + 1) % size) for i in range(size - 1)]
        down = [(j, i) for i, j in up]
        last = lax.slice_in_dim(value, length - width, length, axis=dim)
        first = lax.slice_in_dim(value, 0, width, axis=dim)
        before = lax.ppermute(last, axis, up)
        after = lax.ppermute(first, axis, down)
        value = jnp.concatenate([before, value, after], axis=dim)
    return value


def attend(query_tile, key_tile, value_tile, keep, text_keys, text_values):
    keys_all = jnp.concatenate([key_tile, text_keys], 0)
    vals_all = jnp.concatenate([value_tile, text_values], 0)
    scores = jnp.einsum(
        "qhd,khd->hqk", query_tile, keys_all, preferred_element_type=jnp.float32
    ) * query_tile.shape[2] ** (-0.5)
    allowed = jnp.concatenate([keep, jnp.ones((text_keys.shape[0],), jnp.float32) > 0.5])
    scores = jnp.where(allowed[None, None, :], scores, jnp.float32(-1e30))
    top = jnp.max(scores, -1, keepdims=True)
    weights = jnp.exp(scores - top)
    total = jnp.sum(weights, -1)
    rounded = weights.astype(jnp.bfloat16)
    summed = jnp.einsum("hqk,khd->qhd", rounded, vals_all, preferred_element_type=jnp.float32)
    return (summed / jnp.transpose(total)[:, :, None]).astype(jnp.bfloat16)


def inside_tiles(position, count, devices):
    place = position * count + jnp.arange(count + 2, dtype=jnp.int32) - 1
    return (place >= 0) & (place < count * devices)


def per_device(queries, keys, values, text_keys, text_values):
    width = queries.shape[3] // HEADS
    local_kv = jnp.stack((keys, values))
    heads_here = HEADS
    count_t = queries.shape[0] // TILE_T
    count_h = queries.shape[1] // TILE_H
    count_w = queries.shape[2] // TILE_W
    chans = queries.shape[3]
    shape7 = (count_t, TILE_T, count_h, TILE_H, count_w, TILE_W, chans)
    grid_q = queries.reshape(shape7)
    both = local_kv.reshape((2,) + shape7)
    padded = extended(both, (("ta", 1), ("ha", 3), ("wa", 5)), 1)
    keep_h = inside_tiles(lax.axis_index("ha"), count_h, lax.axis_size("ha"))
    text_pair = jnp.stack((text_keys, text_values))
    text_full = lax.all_gather(text_pair, ("ta", "ha", "wa"), axis=1, tiled=True)
    text_full = text_full.reshape(2, -1, heads_here, width)
    keep_t = inside_tiles(lax.axis_index("ta"), count_t, lax.axis_size("ta"))
    keep_w = inside_tiles(lax.axis_index("wa"), count_w, lax.axis_size("wa"))
    row_list = []
    for tile_b in range(count_h):
        window = padded[:, 0:3, :, tile_b : tile_b + 3, :, 0:3].reshape(2, -1, heads_here, width)
        mask = (
            keep_t[:, None, None, None, None, None]
            & keep_h[tile_b : tile_b + 3][None, None, :, None, None, None]
            & keep_w[None, None, None, None, :, None]
        )
        mask = jnp.broadcast_to(mask, (3, TILE_T, 3, TILE_H, 3, TILE_W)).reshape(-1)
        query_tile = grid_q[0, :, tile_b, :, 0].reshape(-1, heads_here, width)
        result = attend(query_tile, window[0], window[1], mask, text_full[0], text_full[1])
        col_list = [result.reshape(TILE_T, TILE_H, TILE_W, chans)]
        row_list.append(jnp.stack(col_list))
    plane_list = [jnp.stack(row_list)]
    tiles = jnp.stack(plane_list)
    tiles = jnp.transpose(tiles, (0, 3, 1, 4, 2, 5, 6))
    tiles = tiles.reshape(queries.shape)
    return tiles


def solution(mesh):
    placed = (
        P("ta", "ha", "wa", None),
        P("ta", "ha", "wa", None),
        P("ta", "ha", "wa", None),
        P(("ta", "ha", "wa"), None),
        P(("ta", "ha", "wa"), None),
    )
    return jax.shard_map(
        per_device, mesh=mesh, in_specs=placed, out_specs=P("ta", "ha", "wa", None), check_vma=False
    )
```

profile of v0, /device:TPU:0, one launch (start us, length us, event | category | flops | bytes accessed | tf_op | source)
XLA Modules:
  0.0 919.0 jit_solution(13567890914744605254)
XLA Ops:
  2.9 4.6 collective-permute-start
  7.6 32.0 %collective-permute-done.1 = bf16[2,1,4,2,8,1,8,768]{7,6,5,4,3,2,1,0:T(8,128)(2,1)S(1)} collective-permute-done((bf16[2,1,4,2,8,1,8,768]{7,6,5,4,3,2,1,0:T(8,128)(2,1)S(1)}, bf16[2,1,4,2,8,1,8,768]{7,6,5,4,3,2,1,0:T(8,128)(2,1)S(1)}, u32[]{:S(2)}, u32[]{:S(2)}) %collective-permute-start.1) | collective-permute-done | bytes 1572896 | tf_op jit(solution)/shard_map/ppermute | solution.py:20
  45.9 2.7 collective-permute-done.2
  48.6 2.4 collective-permute-done.3
  51.0 4.6 pad_maximum_fusion.9
  56.9 8.2 collective-permute-start.4
  66.8 515.9 %all_gather.3 = bf16[2,256,768]{2,0,1:T(2,128)(2,1)S(1)} all-gather(bf16[2,2,768]{2,0,1:T(2,128)(2,1)S(1)} %copy.51), channel_id=1, replica_groups=mesh['ta'=8,'ha'=2,'wa'=8] {'ta','ha','wa'}, dimensions={1}, use_global_device_ids=true | all-gather | bytes 792576 | tf_op jit(solution)/shard_map/all_gather | solution.py:60
  584.9 2.8 copy.52
  596.2 18.5 %pad_maximum_fusion = bf16[2,3,4,4,8,3,8,768]{7,6,5,4,3,2,1,0:T(8,128)(2,1)} fusion(bf16[2,3,4,4,8,1,8,768]{7,6,5,4,3,2,1,0:T(8,128)(2,1)} %collective-permute-done.5, bf16[2,3,4,1,8,1,8,768]{7,6,5,4,3,2,1,0:T(8,128)(2,1)} %copy-done.3, bf16[2,1,4,2,8,1,8,768]{7,6,5,4,3,2,1,0:T(8,128)(2,1)S(1)} %collective-permute-done.1, ...), kind=kLoop, calls=%fused_computation.12 | loop fusion | flops 99090432 | bytes 56623104 | tf_op jit(solution)/shard_map/concatenate | solution.py:21
  614.7 28.4 %fusion.46 = (bf16[1,3,4,3,8,3,8,768]{7,6,5,4,3,2,1,0:T(8,128)(2,1)}, bf16[1,3,4,3,8,3,8,768]{7,6,5,4,3,2,1,0:T(8,128)(2,1)}, bf16[1,3,4,3,8,3,8,768]{7,6,5,4,3,...) fusion(bf16[2,3,4,4,8,3,8,768]{7,6,5,4,3,2,1,0:T(8,128)(2,1)} %pad_maximum_fusion), kind=kLoop, calls=%fused_computation.57 | loop fusion | bytes 84934656 | tf_op jit(solution)/shard_map/slice | solution.py:74
  643.2 22.2 %squeeze.20 = bf16[6912,6,128]{2,1,0:T(8,128)(2,1)} reshape(bf16[1,3,4,3,8,3,8,768]{7,6,5,4,3,2,1,0:T(8,128)(2,1)} %get-tuple-element.5) | data formatting | bytes 21233664 | tf_op jit(solution)/shard_map/squeeze | solution.py:74
  665.4 17.3 %copy.53 = bf16[6912,6,128]{0,2,1:T(8,128)(2,1)} copy(bf16[6912,6,128]{2,1,0:T(8,128)(2,1)} %squeeze.20) | data formatting | bytes 21233664 | tf_op jit(solution)/shard_map/squeeze | solution.py:74
  682.7 22.2 %squeeze.25 = bf16[6912,6,128]{2,1,0:T(8,128)(2,1)} reshape(bf16[1,3,4,3,8,3,8,768]{7,6,5,4,3,2,1,0:T(8,128)(2,1)} %get-tuple-element.6) | data formatting | bytes 21233664 | tf_op jit(solution)/shard_map/squeeze | solution.py:74
  705.0 11.6 %copy.62 = bf16[6912,6,128]{2,0,1:T(8,128)(2,1)} copy(bf16[6912,6,128]{2,1,0:T(8,128)(2,1)} %squeeze.25) | data formatting | bytes 21233664 | tf_op jit(solution)/shard_map/squeeze | solution.py:74
  716.6 22.2 %squeeze.24 = bf16[6912,6,128]{2,1,0:T(8,128)(2,1)} reshape(bf16[1,3,4,3,8,3,8,768]{7,6,5,4,3,2,1,0:T(8,128)(2,1)} %get-tuple-element.7) | data formatting | bytes 21233664 | tf_op jit(solution)/shard_map/squeeze | solution.py:74
  738.8 17.2 %copy.61 = bf16[6912,6,128]{0,2,1:T(8,128)(2,1)} copy(bf16[6912,6,128]{2,1,0:T(8,128)(2,1)} %squeeze.24) | data formatting | bytes 21233664 | tf_op jit(solution)/shard_map/squeeze | solution.py:74
  756.1 22.2 %squeeze.22 = bf16[6912,6,128]{2,1,0:T(8,128)(2,1)} reshape(bf16[1,3,4,3,8,3,8,768]{7,6,5,4,3,2,1,0:T(8,128)(2,1)} %get-tuple-element.8) | data formatting | bytes 21233664 | tf_op jit(solution)/shard_map/squeeze | solution.py:74
  778.3 11.8 %copy.55 = bf16[6912,6,128]{2,0,1:T(8,128)(2,1)} copy(bf16[6912,6,128]{2,1,0:T(8,128)(2,1)} %squeeze.22) | data formatting | bytes 21233664 | tf_op jit(solution)/shard_map/squeeze | solution.py:74
  790.1 22.6 %bitcast_reduce_fusion.1 = (f32[6,256]{1,0:T(8,128)S(1)}, f32[6,7168,256]{2,1,0:T(8,128)}) fusion(pred[7168]{0:T(1024)(128)(4,1)S(1)} %concatenate.32, bf16[256,6,128]{2,1,0:T(8,128)(2,1)S(1)} %copy-done.5, bf16[256,6,128]{2,0,1:T(8,128)(2,1)S(1)} %copy-done.6, bf16[6912,6,128]{2,0,1:T(8,128)(2,1)} %copy.55), kind=kOutput, calls=%fused_computation.4 | convolution fusion | flops 2873620992 | bytes 55456768 | tf_op jit(solution)/shard_map/qhd,khd->hqk/dot_general | solution.py:28
  812.8 19.5 %fusion.2 = f32[6,256]{1,0:T(8,128)S(1)} fusion(f32[6,7168,256]{2,1,0:T(8,128)} %get-tuple-element.24, f32[6,256]{1,0:T(8,128)S(1)} %get-tuple-element.23, pred[7168]{0:T(1024)(128)(4,1)S(1)} %concatenate.32), kind=kLoop, calls=%fused_computation.8 | loop fusion | flops 44038656 | bytes 44059648 | tf_op jit(solution)/shard_map/reduce_sum | solution.py:35
  832.3 20.9 %fusion.33 = bf16[256,6,128]{0,2,1:T(8,128)(2,1)S(1)} fusion(f32[6,7168,256]{2,1,0:T(8,128)} %get-tuple-element.24, f32[6,256]{1,0:T(8,128)S(1)} %get-tuple-element.23, pred[7168]{0:T(1024)(128)(4,1)S(1)} %concatenate.32, bf16[256,6,128]{0,2,1:T(8,128)(2,1)S(1)} %bitcast.92, bf16[6912,6,128]{0,2,1:T(8,128)(2,1)} %copy.53, f32[256,6]{0,1:T(8,128)S(1)} %bitcast.95), kind=kOutput, calls=%fused_computation.35 | convolution fusion | flops 2885025792 | bytes 55462912 | tf_op jit(solution)/shard_map/hqk,khd->qhd/dot_general | solution.py:37
  854.1 22.7 %bitcast_reduce_fusion = (f32[6,256]{1,0:T(8,128)S(1)}, f32[6,7168,256]{2,1,0:T(8,128)}) fusion(pred[7168]{0:T(1024)(128)(4,1)S(1)} %copy-done.8, bf16[256,6,128]{2,1,0:T(8,128)(2,1)S(1)} %copy-done.4, bf16[256,6,128]{2,0,1:T(8,128)(2,1)S(1)} %copy-done.6, bf16[6912,6,128]{2,0,1:T(8,128)(2,1)} %copy.62), kind=kOutput, calls=%fused_computation.1 | convolution fusion | flops 2873620992 | bytes 55456768 | tf_op jit(solution)/shard_map/qhd,khd->hqk/dot_general | solution.py:28
  876.8 19.5 %fusion.4 = f32[6,256]{1,0:T(8,128)S(1)} fusion(f32[6,7168,256]{2,1,0:T(8,128)} %get-tuple-element.22, f32[6,256]{1,0:T(8,128)S(1)} %get-tuple-element.21, pred[7168]{0:T(1024)(128)(4,1)S(1)} %copy-done.8), kind=kLoop, calls=%fused_computation.10 | loop fusion | flops 44038656 | bytes 44059648 | tf_op jit(solution)/shard_map/reduce_sum | solution.py:35
  896.3 20.9 %fusion.27 = bf16[256,6,128]{0,2,1:T(8,128)(2,1)S(1)} fusion(f32[6,7168,256]{2,1,0:T(8,128)} %get-tuple-element.22, f32[6,256]{1,0:T(8,128)S(1)} %get-tuple-element.21, pred[7168]{0:T(1024)(128)(4,1)S(1)} %copy-done.8, bf16[256,6,128]{0,2,1:T(8,128)(2,1)S(1)} %bitcast.93, bf16[6912,6,128]{0,2,1:T(8,128)(2,1)} %copy.61, f32[256,6]{0,1:T(8,128)S(1)} %bitcast.94), kind=kOutput, calls=%fused_computation.33 | convolution fusion | flops 2885025792 | bytes 55462912 | tf_op jit(solution)/shard_map/hqk,khd->qhd/dot_general | solution.py:37
  (57 shorter events, 25.5 us)
Async XLA Ops:
  0.0 51.0 %copy-start = (bf16[4,16,8,768]{3,2,1,0:T(8,128)(2,1)S(1)}, bf16[4,16,8,768]{3,2,1,0:T(8,128)(2,1)}, u32[]{:S(2)}) copy-start(bf16[4,16,8,768]{3,2,1,0:T(8,128)(2,1)} %param.7) | copy-start | bytes 2359300
  0.0 51.0 %copy-start.1 = (bf16[4,16,8,768]{3,2,1,0:T(8,128)(2,1)S(1)}, bf16[4,16,8,768]{3,2,1,0:T(8,128)(2,1)}, u32[]{:S(2)}) copy-start(bf16[4,16,8,768]{3,2,1,0:T(8,128)(2,1)} %param.6) | copy-start | bytes 2359300
  1.6 38.0 %collective-permute-start.1 = (bf16[2,1,4,2,8,1,8,768]{7,6,5,4,3,2,1,0:T(8,128)(2,1)S(1)}, bf16[2,1,4,2,8,1,8,768]{7,6,5,4,3,2,1,0:T(8,128)(2,1)S(1)}, u32[]{:S(2)}, u32[]{:S(2)}) collective-permute-start(bf16[2,1,4,2,8,1,8,768]{7,6,5,4,3,2,1,0:T(8,128)(2,1)S(1)} %pad_maximum_fusion.11), channel_id=1, source_target_pairs={{16,0},{32,16},{48,32},{64,48},{80,64},{96,80},{112,96},{17,1},{33... | collective-permute-start | bytes 4718600 | tf_op jit(solution)/shard_map/ppermute | solution.py:20
  2.9 37.8 %collective-permute-start = (bf16[2,1,4,2,8,1,8,768]{7,6,5,4,3,2,1,0:T(8,128)(2,1)S(1)}, bf16[2,1,4,2,8,1,8,768]{7,6,5,4,3,2,1,0:T(8,128)(2,1)S(1)}, u32[]{:S(2)}, u32[]{:S(2)}) collective-permute-start(bf16[2,1,4,2,8,1,8,768]{7,6,5,4,3,2,1,0:T(8,128)(2,1)S(1)} %pad_maximum_fusion.11), channel_id=1, source_target_pairs={{0,16},{16,32},{32,48},{48,64},{64,80},{80,96},{96,112},{1,17},{17... | collective-permute-start | bytes 4718600 | tf_op jit(solution)/shard_map/ppermute | solution.py:19
  43.0 22.1 %copy-start.9 = (bf16[2,768]{1,0:T(2,128)(2,1)S(1)}, bf16[2,768]{1,0:T(2,128)(2,1)}, u32[]{:S(2)}) copy-start(bf16[2,768]{1,0:T(2,128)(2,1)} %param.9) | copy-start | bytes 9220
  43.0 22.1 %copy-start.10 = (bf16[2,768]{1,0:T(2,128)(2,1)S(1)}, bf16[2,768]{1,0:T(2,128)(2,1)}, u32[]{:S(2)}) copy-start(bf16[2,768]{1,0:T(2,128)(2,1)} %param.8) | copy-start | bytes 9220
  43.0 5.6 collective-permute-start.2
  44.6 6.4 collective-permute-start.3
  48.6 7.0 copy-start.2
  51.0 5.8 copy-start.3
  55.6 540.6 %collective-permute-start.5 = (bf16[2,3,4,4,8,1,8,768]{7,6,5,4,3,2,1,0:T(8,128)(2,1)}, bf16[2,3,4,4,8,1,8,768]{7,6,5,4,3,2,1,0:T(8,128)(2,1)}, u32[]{:S(2)}, u32[]{:S(2)}) collective-permute-start(bf16[2,3,4,4,8,1,8,768]{7,6,5,4,3,2,1,0:T(8,128)(2,1)} %pad_maximum_fusion.9), channel_id=1, source_target_pairs={{1,0},{2,1},{3,2},{4,3},{5,4},{6,5},{7,6},{9,8},{10,9},{11,10},{12... | collective-permute-start | bytes 28311560 | tf_op jit(solution)/shard_map/ppermute | solution.py:20
  56.9 539.3 %collective-permute-start.4 = (bf16[2,3,4,4,8,1,8,768]{7,6,5,4,3,2,1,0:T(8,128)(2,1)}, bf16[2,3,4,4,8,1,8,768]{7,6,5,4,3,2,1,0:T(8,128)(2,1)}, u32[]{:S(2)}, u32[]{:S(2)}) collective-permute-start(bf16[2,3,4,4,8,1,8,768]{7,6,5,4,3,2,1,0:T(8,128)(2,1)} %pad_maximum_fusion.9), channel_id=1, source_target_pairs={{0,1},{1,2},{2,3},{3,4},{4,5},{5,6},{6,7},{8,9},{9,10},{10,11},{11... | collective-permute-start | bytes 28311560 | tf_op jit(solution)/shard_map/ppermute | solution.py:19
  778.3 11.8 %copy-start.5 = (bf16[256,6,128]{2,1,0:T(8,128)(2,1)S(1)}, bf16[256,6,128]{2,1,0:T(8,128)(2,1)}, u32[]{:S(2)}) copy-start(bf16[256,6,128]{2,1,0:T(8,128)(2,1)} %reshape_squeeze.6) | copy-start | bytes 1179652
  778.3 11.8 %copy-start.6 = (bf16[256,6,128]{2,0,1:T(8,128)(2,1)S(1)}, bf16[256,6,128]{2,0,1:T(8,128)(2,1)}, u32[]{:S(2)}) copy-start(bf16[256,6,128]{2,0,1:T(8,128)(2,1)} %copy.56) | copy-start | bytes 1179652
  812.8 19.5 %copy-start.7 = (bf16[1,256,768]{1,2,0:T(8,128)(2,1)S(1)}, bf16[1,256,768]{1,2,0:T(8,128)(2,1)}, u32[]{:S(2)}) copy-start(bf16[1,256,768]{1,2,0:T(8,128)(2,1)} %copy.52) | copy-start | bytes 1179652
  832.3 21.8 %copy-start.4 = (bf16[256,6,128]{2,1,0:T(8,128)(2,1)S(1)}, bf16[256,6,128]{2,1,0:T(8,128)(2,1)}, u32[]{:S(2)}) copy-start(bf16[256,6,128]{2,1,0:T(8,128)(2,1)} %reshape_squeeze.7) | copy-start | bytes 1179652
  832.3 21.8 %copy-start.8 = (pred[7168]{0:T(1024)(128)(4,1)S(1)}, pred[7168]{0:T(1024)(128)(4,1)}, u32[]{:S(2)}) copy-start(pred[7168]{0:T(1024)(128)(4,1)} %concatenate.35) | copy-start | bytes 21508
where the time goes:
time: 923 us; the launch traced here: 919 us
  blocking collectives  516 us (56%)
  local copies, waits for them, and re-layouts  193 us (21%)
  matrix products  87.1 us (9%)
  other arithmetic  65.7 us (7%)
  waiting for transfers between devices  38.3 us (4%)
  starting transfers between devices  18.3 us (2%)
    all_gather x1, blocking collectives, per_device(): lax.all_gather(text_pair, ('ta', 'ha', 'wa'), axis=1, tiled=True)  516 us
    squeeze x4, local copies, waits for them, and re-layouts, per_device(): window[1]  79.1 us
    squeeze x4, local copies, waits for them, and re-layouts, per_device(): window[0]  67.9 us
    dot_general x2, matrix products, attend(): jnp.einsum('qhd,khd->hqk', query_tile, keys_all, preferred_element_type=j...  45.3 us
    dot_general x2, matrix products, attend(): jnp.einsum('hqk,khd->qhd', rounded, vals_all, preferred_element_type=jnp....  41.8 us
    reduce_sum x2, other arithmetic, attend(): total = jnp.sum(weights, -1)  39 us
    ppermute x3, waiting for transfers between devices, extended(): after = lax.ppermute(first, axis, down)  34.4 us
    slice x1, local copies, waits for them, and re-layouts, per_device(): window[1]  28.4 us
  transfers between devices with their start and end apart: 6, of which 4 were waited for; matrix products, arithmetic and copies ran while one was open for 2% of the time, Pallas kernels for 0%

commit v1 on v0

--- a/solution.py
+++ b/solution.py
@@ -57,7 +57,16 @@
     padded = extended(both, (("ta", 1), ("ha", 3), ("wa", 5)), 1)
     keep_h = inside_tiles(lax.axis_index("ha"), count_h, lax.axis_size("ha"))
     text_pair = jnp.stack((text_keys, text_values))
-    text_full = lax.all_gather(text_pair, ("ta", "ha", "wa"), axis=1, tiled=True)
+    scales_define = lambda vec, dimension_no: jnp.concatenate(
+        lax.all_to_all(
+            jnp.stack([vec for _ in range(lax.axis_size(("ta", "ha", "wa")))], 0),
+            ("ta", "ha", "wa"),
+            0,
+            0,
+        ),
+        dimension_no,
+    )
+    text_full = scales_define(text_pair, 1)
     text_full = text_full.reshape(2, -1, heads_here, width)
     keep_t = inside_tiles(lax.axis_index("ta"), count_t, lax.axis_size("ta"))
     keep_w = inside_tiles(lax.axis_index("wa"), count_w, lax.axis_size("wa"))

time: 923 us -> 625 us (0.68)
  blocking collectives: 516 us -> 0 us
  waiting for transfers between devices: 38.3 us -> 238 us
  starting transfers between devices: 18.3 us -> 34.6 us
    all_gather x1 -> x0, blocking collectives: 516 us -> none  [per_device(): lax.all_gather(text_pair, ('ta', 'ha', 'wa'), axis=1, tiled=True)]
    all_to_all x0 -> x1, waiting for transfers between devices: none -> 199 us  [per_device(): lax.all_to_all(jnp.stack([vec for _ in range(lax.axis_size(('ta', 'ha', '...]
    all_to_all x0 -> x1, starting transfers between devices: none -> 16.3 us  [per_device(): lax.all_to_all(jnp.stack([vec for _ in range(lax.axis_size(('ta', 'ha', '...]
  transfers between devices with their start and end apart: 6 -> 7, of which waited for: 4 -> 5; matrix products, arithmetic and copies ran while one was open for 2% -> 3% of each run, Pallas kernels for 0% -> 0%
where the time goes in v1:
time: 625 us; the launch traced here: 620 us
  waiting for transfers between devices  238 us (38%)
  local copies, waits for them, and re-layouts  195 us (31%)
  matrix products  86.9 us (14%)
  other arithmetic  65.6 us (10%)
  starting transfers between devices  34.6 us (6%)
    all_to_all x1, waiting for transfers between devices, per_device(): lax.all_to_all(jnp.stack([vec for _ in range(lax.axis_size(('ta', 'ha', '...  199 us
    squeeze x4, local copies, waits for them, and re-layouts, per_device(): window[1]  79 us
    squeeze x4, local copies, waits for them, and re-layouts, per_device(): window[0]  67.8 us
    dot_general x2, matrix products, attend(): jnp.einsum('qhd,khd->hqk', query_tile, keys_all, preferred_element_type=j...  45.1 us
    dot_general x2, matrix products, attend(): jnp.einsum('hqk,khd->qhd', rounded, vals_all, preferred_element_type=jnp....  41.8 us
    reduce_sum x2, other arithmetic, attend(): total = jnp.sum(weights, -1)  39 us
    ppermute x3, waiting for transfers between devices, extended(): after = lax.ppermute(first, axis, down)  34.4 us
    slice x1, local copies, waits for them, and re-layouts, per_device(): window[1]  28.4 us
  transfers between devices with their start and end apart: 7, of which 5 were waited for; matrix products, arithmetic and copies ran while one was open for 3% of the time, Pallas kernels for 0%

profile of v1, /device:TPU:0, one launch (start us, length us, event | category | flops | bytes accessed | tf_op | source)
XLA Modules:
  0.0 620.0 jit_solution(335027535919874556)
XLA Ops:
  2.9 4.6 collective-permute-start
  7.6 32.0 %collective-permute-done.1 = bf16[2,1,4,2,8,1,8,768]{7,6,5,4,3,2,1,0:T(8,128)(2,1)S(1)} collective-permute-done((bf16[2,1,4,2,8,1,8,768]{7,6,5,4,3,2,1,0:T(8,128)(2,1)S(1)}, bf16[2,1,4,2,8,1,8,768]{7,6,5,4,3,2,1,0:T(8,128)(2,1)S(1)}, u32[]{:S(2)}, u32[]{:S(2)}) %collective-permute-start.1) | collective-permute-done | bytes 1572896 | tf_op jit(solution)/shard_map/ppermute | solution.py:20
  45.9 2.7 collective-permute-done.2
  48.6 2.4 collective-permute-done.3
  51.0 4.5 pad_maximum_fusion.9
  56.8 8.2 %collective-permute-start.4 = (bf16[2,3,4,4,8,1,8,768]{7,6,5,4,3,2,1,0:T(8,128)(2,1)}, bf16[2,3,4,4,8,1,8,768]{7,6,5,4,3,2,1,0:T(8,128)(2,1)}, u32[]{:S(2)}, u32[]{:S(2)}) collective-permute-start(bf16[2,3,4,4,8,1,8,768]{7,6,5,4,3,2,1,0:T(8,128)(2,1)} %pad_maximum_fusion.9), channel_id=1, source_target_pairs={{0,1},{1,2},{2,3},{3,4},{4,5},{5,6},{6,7},{8,9},{9,10},{10,11},{11... | collective-permute-start | bytes 28311560 | tf_op jit(solution)/shard_map/ppermute | solution.py:19
  66.3 16.3 %all-to-all-start = ((bf16[128,2,2,768]{3,2,1,0:T(2,128)(2,1)}), bf16[128,2,2,768]{3,2,1,0:T(2,128)(2,1)}, u32[]{:S(2)}, u32[]{:S(2)}) async-start(bf16[128,2,2,768]{3,2,1,0:T(2,128)(2,1)} %stack.24), calls=%async_computation | async-start | bytes 1572864 | tf_op jit(solution)/shard_map/all_to_all | solution.py:61
  89.8 199.2 %all-to-all-done = bf16[128,2,2,768]{3,2,1,0:T(2,128)(2,1)} async-done(((bf16[128,2,2,768]{3,2,1,0:T(2,128)(2,1)}), bf16[128,2,2,768]{3,2,1,0:T(2,128)(2,1)}, u32[]{:S(2)}, u32[]{:S(2)}) %all-to-all-start) | async-done | bytes 786464 | tf_op jit(solution)/shard_map/all_to_all | solution.py:61
  297.7 18.4 %pad_maximum_fusion = bf16[2,3,4,4,8,3,8,768]{7,6,5,4,3,2,1,0:T(8,128)(2,1)} fusion(bf16[2,3,4,4,8,1,8,768]{7,6,5,4,3,2,1,0:T(8,128)(2,1)} %collective-permute-done.5, bf16[2,3,4,1,8,1,8,768]{7,6,5,4,3,2,1,0:T(8,128)(2,1)} %copy-done.3, bf16[2,1,4,2,8,1,8,768]{7,6,5,4,3,2,1,0:T(8,128)(2,1)S(1)} %collective-permute-done.1, ...), kind=kLoop, calls=%fused_computation.12 | loop fusion | flops 99090432 | bytes 56623104 | tf_op jit(solution)/shard_map/concatenate | solution.py:21
  316.1 28.4 %fusion.46 = (bf16[1,3,4,3,8,3,8,768]{7,6,5,4,3,2,1,0:T(8,128)(2,1)}, bf16[1,3,4,3,8,3,8,768]{7,6,5,4,3,2,1,0:T(8,128)(2,1)}, bf16[1,3,4,3,8,3,8,768]{7,6,5,4,3,...) fusion(bf16[2,3,4,4,8,3,8,768]{7,6,5,4,3,2,1,0:T(8,128)(2,1)} %pad_maximum_fusion), kind=kLoop, calls=%fused_computation.57 | loop fusion | bytes 84934656 | tf_op jit(solution)/shard_map/slice | solution.py:83
  344.5 22.2 %squeeze.20 = bf16[6912,6,128]{2,1,0:T(8,128)(2,1)} reshape(bf16[1,3,4,3,8,3,8,768]{7,6,5,4,3,2,1,0:T(8,128)(2,1)} %get-tuple-element.5) | data formatting | bytes 21233664 | tf_op jit(solution)/shard_map/squeeze | solution.py:83
  366.7 17.3 %copy.51 = bf16[6912,6,128]{0,2,1:T(8,128)(2,1)} copy(bf16[6912,6,128]{2,1,0:T(8,128)(2,1)} %squeeze.20) | data formatting | bytes 21233664 | tf_op jit(solution)/shard_map/squeeze | solution.py:83
  384.0 22.2 %squeeze.25 = bf16[6912,6,128]{2,1,0:T(8,128)(2,1)} reshape(bf16[1,3,4,3,8,3,8,768]{7,6,5,4,3,2,1,0:T(8,128)(2,1)} %get-tuple-element.6) | data formatting | bytes 21233664 | tf_op jit(solution)/shard_map/squeeze | solution.py:83
  406.2 11.6 %copy.61 = bf16[6912,6,128]{2,0,1:T(8,128)(2,1)} copy(bf16[6912,6,128]{2,1,0:T(8,128)(2,1)} %squeeze.25) | data formatting | bytes 21233664 | tf_op jit(solution)/shard_map/squeeze | solution.py:83
  417.9 22.2 %squeeze.24 = bf16[6912,6,128]{2,1,0:T(8,128)(2,1)} reshape(bf16[1,3,4,3,8,3,8,768]{7,6,5,4,3,2,1,0:T(8,128)(2,1)} %get-tuple-element.7) | data formatting | bytes 21233664 | tf_op jit(solution)/shard_map/squeeze | solution.py:83
  440.1 17.2 %copy.59 = bf16[6912,6,128]{0,2,1:T(8,128)(2,1)} copy(bf16[6912,6,128]{2,1,0:T(8,128)(2,1)} %squeeze.24) | data formatting | bytes 21233664 | tf_op jit(solution)/shard_map/squeeze | solution.py:83
  457.3 22.2 %squeeze.22 = bf16[6912,6,128]{2,1,0:T(8,128)(2,1)} reshape(bf16[1,3,4,3,8,3,8,768]{7,6,5,4,3,2,1,0:T(8,128)(2,1)} %get-tuple-element.8) | data formatting | bytes 21233664 | tf_op jit(solution)/shard_map/squeeze | solution.py:83
  479.6 11.7 %copy.53 = bf16[6912,6,128]{2,0,1:T(8,128)(2,1)} copy(bf16[6912,6,128]{2,1,0:T(8,128)(2,1)} %squeeze.22) | data formatting | bytes 21233664 | tf_op jit(solution)/shard_map/squeeze | solution.py:83
  491.3 22.4 %bitcast_reduce_fusion.1 = (f32[6,256]{1,0:T(8,128)S(1)}, f32[6,7168,256]{2,1,0:T(8,128)}) fusion(pred[7168]{0:T(1024)(128)(4,1)S(1)} %concatenate.32, bf16[256,6,128]{2,1,0:T(8,128)(2,1)S(1)} %copy-done.5, bf16[256,6,128]{2,0,1:T(8,128)(2,1)S(1)} %copy.54, bf16[6912,6,128]{2,0,1:T(8,128)(2,1)} %copy.53), kind=kOutput, calls=%fused_computation.4 | convolution fusion | flops 2873620992 | bytes 55456768 | tf_op jit(solution)/shard_map/qhd,khd->hqk/dot_general | solution.py:28
  513.7 19.5 %fusion.2 = f32[6,256]{1,0:T(8,128)S(1)} fusion(f32[6,7168,256]{2,1,0:T(8,128)} %get-tuple-element.24, f32[6,256]{1,0:T(8,128)S(1)} %get-tuple-element.23, pred[7168]{0:T(1024)(128)(4,1)S(1)} %concatenate.32), kind=kLoop, calls=%fused_computation.8 | loop fusion | flops 44038656 | bytes 44059648 | tf_op jit(solution)/shard_map/reduce_sum | solution.py:35
  533.3 20.9 %fusion.33 = bf16[256,6,128]{0,2,1:T(8,128)(2,1)S(1)} fusion(f32[6,7168,256]{2,1,0:T(8,128)} %get-tuple-element.24, f32[6,256]{1,0:T(8,128)S(1)} %get-tuple-element.23, pred[7168]{0:T(1024)(128)(4,1)S(1)} %concatenate.32, bf16[256,6,128]{0,2,1:T(8,128)(2,1)S(1)} %copy-done.6, bf16[6912,6,128]{0,2,1:T(8,128)(2,1)} %copy.51, f32[256,6]{0,1:T(8,128)S(1)} %bitcast.95), kind=kOutput, calls=%fused_computation.35 | convolution fusion | flops 2885025792 | bytes 55462912 | tf_op jit(solution)/shard_map/hqk,khd->qhd/dot_general | solution.py:37
  555.1 22.7 %bitcast_reduce_fusion = (f32[6,256]{1,0:T(8,128)S(1)}, f32[6,7168,256]{2,1,0:T(8,128)}) fusion(pred[7168]{0:T(1024)(128)(4,1)S(1)} %copy-done.7, bf16[256,6,128]{2,1,0:T(8,128)(2,1)S(1)} %copy-done.4, bf16[256,6,128]{2,0,1:T(8,128)(2,1)S(1)} %copy.54, bf16[6912,6,128]{2,0,1:T(8,128)(2,1)} %copy.61), kind=kOutput, calls=%fused_computation.1 | convolution fusion | flops 2873620992 | bytes 55456768 | tf_op jit(solution)/shard_map/qhd,khd->hqk/dot_general | solution.py:28
  577.7 19.5 %fusion.4 = f32[6,256]{1,0:T(8,128)S(1)} fusion(f32[6,7168,256]{2,1,0:T(8,128)} %get-tuple-element.22, f32[6,256]{1,0:T(8,128)S(1)} %get-tuple-element.21, pred[7168]{0:T(1024)(128)(4,1)S(1)} %copy-done.7), kind=kLoop, calls=%fused_computation.10 | loop fusion | flops 44038656 | bytes 44059648 | tf_op jit(solution)/shard_map/reduce_sum | solution.py:35
  597.2 20.9 %fusion.27 = bf16[256,6,128]{0,2,1:T(8,128)(2,1)S(1)} fusion(f32[6,7168,256]{2,1,0:T(8,128)} %get-tuple-element.22, f32[6,256]{1,0:T(8,128)S(1)} %get-tuple-element.21, pred[7168]{0:T(1024)(128)(4,1)S(1)} %copy-done.7, bf16[256,6,128]{0,2,1:T(8,128)(2,1)S(1)} %copy-done.6, bf16[6912,6,128]{0,2,1:T(8,128)(2,1)} %copy.59, f32[256,6]{0,1:T(8,128)S(1)} %bitcast.94), kind=kOutput, calls=%fused_computation.33 | convolution fusion | flops 2885025792 | bytes 55462912 | tf_op jit(solution)/shard_map/hqk,khd->qhd/dot_general | solution.py:37
  (57 shorter events, 30.1 us)
Async XLA Ops:
  0.0 51.0 %copy-start = (bf16[4,16,8,768]{3,2,1,0:T(8,128)(2,1)S(1)}, bf16[4,16,8,768]{3,2,1,0:T(8,128)(2,1)}, u32[]{:S(2)}) copy-start(bf16[4,16,8,768]{3,2,1,0:T(8,128)(2,1)} %param.7) | copy-start | bytes 2359300
  0.0 51.0 %copy-start.1 = (bf16[4,16,8,768]{3,2,1,0:T(8,128)(2,1)S(1)}, bf16[4,16,8,768]{3,2,1,0:T(8,128)(2,1)}, u32[]{:S(2)}) copy-start(bf16[4,16,8,768]{3,2,1,0:T(8,128)(2,1)} %param.6) | copy-start | bytes 2359300
  1.6 38.0 %collective-permute-start.1 = (bf16[2,1,4,2,8,1,8,768]{7,6,5,4,3,2,1,0:T(8,128)(2,1)S(1)}, bf16[2,1,4,2,8,1,8,768]{7,6,5,4,3,2,1,0:T(8,128)(2,1)S(1)}, u32[]{:S(2)}, u32[]{:S(2)}) collective-permute-start(bf16[2,1,4,2,8,1,8,768]{7,6,5,4,3,2,1,0:T(8,128)(2,1)S(1)} %pad_maximum_fusion.11), channel_id=1, source_target_pairs={{16,0},{32,16},{48,32},{64,48},{80,64},{96,80},{112,96},{17,1},{33... | collective-permute-start | bytes 4718600 | tf_op jit(solution)/shard_map/ppermute | solution.py:20
  2.9 37.8 %collective-permute-start = (bf16[2,1,4,2,8,1,8,768]{7,6,5,4,3,2,1,0:T(8,128)(2,1)S(1)}, bf16[2,1,4,2,8,1,8,768]{7,6,5,4,3,2,1,0:T(8,128)(2,1)S(1)}, u32[]{:S(2)}, u32[]{:S(2)}) collective-permute-start(bf16[2,1,4,2,8,1,8,768]{7,6,5,4,3,2,1,0:T(8,128)(2,1)S(1)} %pad_maximum_fusion.11), channel_id=1, source_target_pairs={{0,16},{16,32},{32,48},{48,64},{64,80},{80,96},{96,112},{1,17},{17... | collective-permute-start | bytes 4718600 | tf_op jit(solution)/shard_map/ppermute | solution.py:19
  43.0 22.0 %copy-start.8 = (bf16[2,768]{1,0:T(2,128)(2,1)S(1)}, bf16[2,768]{1,0:T(2,128)(2,1)}, u32[]{:S(2)}) copy-start(bf16[2,768]{1,0:T(2,128)(2,1)} %param.9) | copy-start | bytes 9220
  43.0 22.0 %copy-start.9 = (bf16[2,768]{1,0:T(2,128)(2,1)S(1)}, bf16[2,768]{1,0:T(2,128)(2,1)}, u32[]{:S(2)}) copy-start(bf16[2,768]{1,0:T(2,128)(2,1)} %param.8) | copy-start | bytes 9220
  43.0 5.6 collective-permute-start.2
  44.6 6.4 %collective-permute-start.3 = (bf16[2,3,4,1,8,1,8,768]{7,6,5,4,3,2,1,0:T(8,128)(2,1)S(1)}, bf16[2,3,4,1,8,1,8,768]{7,6,5,4,3,2,1,0:T(8,128)(2,1)S(1)}, u32[]{:S(2)}, u32[]{:S(2)}) collective-permute-start(bf16[2,3,4,1,8,1,8,768]{7,6,5,4,3,2,1,0:T(8,128)(2,1)S(1)} %get-tuple-element.10), channel_id=1, source_target_pairs={{8,0},{9,1},{10,2},{11,3},{12,4},{13,5},{14,6},{15,7},{24,16},{25,... | collective-permute-start | bytes 7077896 | tf_op jit(solution)/shard_map/ppermute | solution.py:20
  48.6 6.9 %copy-start.2 = (bf16[2,3,4,1,8,1,8,768]{7,6,5,4,3,2,1,0:T(8,128)(2,1)}, bf16[2,3,4,1,8,1,8,768]{7,6,5,4,3,2,1,0:T(8,128)(2,1)S(1)}, u32[]{:S(2)}) copy-start(bf16[2,3,4,1,8,1,8,768]{7,6,5,4,3,2,1,0:T(8,128)(2,1)S(1)} %collective-permute-done.2) | copy-start | bytes 7077892
  51.0 5.8 copy-start.3
  55.5 242.1 %collective-permute-start.5 = (bf16[2,3,4,4,8,1,8,768]{7,6,5,4,3,2,1,0:T(8,128)(2,1)}, bf16[2,3,4,4,8,1,8,768]{7,6,5,4,3,2,1,0:T(8,128)(2,1)}, u32[]{:S(2)}, u32[]{:S(2)}) collective-permute-start(bf16[2,3,4,4,8,1,8,768]{7,6,5,4,3,2,1,0:T(8,128)(2,1)} %pad_maximum_fusion.9), channel_id=1, source_target_pairs={{1,0},{2,1},{3,2},{4,3},{5,4},{6,5},{7,6},{9,8},{10,9},{11,10},{12... | collective-permute-start | bytes 28311560 | tf_op jit(solution)/shard_map/ppermute | solution.py:20
  56.8 240.8 %collective-permute-start.4 = (bf16[2,3,4,4,8,1,8,768]{7,6,5,4,3,2,1,0:T(8,128)(2,1)}, bf16[2,3,4,4,8,1,8,768]{7,6,5,4,3,2,1,0:T(8,128)(2,1)}, u32[]{:S(2)}, u32[]{:S(2)}) collective-permute-start(bf16[2,3,4,4,8,1,8,768]{7,6,5,4,3,2,1,0:T(8,128)(2,1)} %pad_maximum_fusion.9), channel_id=1, source_target_pairs={{0,1},{1,2},{2,3},{3,4},{4,5},{5,6},{6,7},{8,9},{9,10},{10,11},{11... | collective-permute-start | bytes 28311560 | tf_op jit(solution)/shard_map/ppermute | solution.py:19
  66.3 222.6 %all-to-all-start = ((bf16[128,2,2,768]{3,2,1,0:T(2,128)(2,1)}), bf16[128,2,2,768]{3,2,1,0:T(2,128)(2,1)}, u32[]{:S(2)}, u32[]{:S(2)}) async-start(bf16[128,2,2,768]{3,2,1,0:T(2,128)(2,1)} %stack.24), calls=%async_computation | async-start | bytes 1572864 | tf_op jit(solution)/shard_map/all_to_all | solution.py:61
  479.6 11.7 %copy-start.5 = (bf16[256,6,128]{2,1,0:T(8,128)(2,1)S(1)}, bf16[256,6,128]{2,1,0:T(8,128)(2,1)}, u32[]{:S(2)}) copy-start(bf16[256,6,128]{2,1,0:T(8,128)(2,1)} %reshape_squeeze.6) | copy-start | bytes 1179652
  513.7 19.5 %copy-start.6 = (bf16[256,6,128]{0,2,1:T(8,128)(2,1)S(1)}, bf16[256,6,128]{0,2,1:T(8,128)(2,1)}, u32[]{:S(2)}) copy-start(bf16[256,6,128]{0,2,1:T(8,128)(2,1)} %copy.52) | copy-start | bytes 1179652
  533.3 21.8 %copy-start.4 = (bf16[256,6,128]{2,1,0:T(8,128)(2,1)S(1)}, bf16[256,6,128]{2,1,0:T(8,128)(2,1)}, u32[]{:S(2)}) copy-start(bf16[256,6,128]{2,1,0:T(8,128)(2,1)} %reshape_squeeze.7) | copy-start | bytes 1179652
  533.3 21.8 %copy-start.7 = (pred[7168]{0:T(1024)(128)(4,1)S(1)}, pred[7168]{0:T(1024)(128)(4,1)}, u32[]{:S(2)}) copy-start(pred[7168]{0:T(1024)(128)(4,1)} %concatenate.35) | copy-start | bytes 21508
